TPU v7x, 32 devices: a whole 2x2x4 slice. The times are simulated.
32 devices in a mesh: dp: 4 (over y, core), row: 2 (over x), col: 4 (over z).
Axes of the slice: x: 2, y: 2, z: 4, core: 2. Of those that a mesh axis runs over, the one named last changes fastest.
Arguments:
- layer_input: bfloat16 [12288, 1536], P(('dp', 'col'), 'row'), may hold values from -6 to 6
- attn_gain: float32 [1536], P('row'), may hold values from 0.25 to 1.75
- qkv_weight: bfloat16 [1536, 4608], P('row', 'col'), may hold values from -0.15625 to 0.15625
- forget_weight: bfloat16 [1536, 24], P('row', 'col'), may hold values from -0.15625 to 0.15625
- forget_bias: float32 [24], P('col'), may hold values from 2.5 to 7
- out_weight: bfloat16 [1536, 1536], P('col', 'row'), may hold values from -0.625 to 0.625
- ffn_gain: float32 [1536], P('row'), may hold values from 0.25 to 1.75
- gate_weight: bfloat16 [1536, 4096], P('row', 'col'), may hold values from -0.15625 to 0.15625
- up_weight: bfloat16 [1536, 4096], P('row', 'col'), may hold values from -0.15625 to 0.15625
- down_weight: bfloat16 [4096, 1536], P('col', 'row'), may hold values from -0.09375 to 0.09375
- prompt_doc: int32 [8, 1024], P(('dp', 'row')), may hold values from 0 to 3, never falling along the last dimension, each value on 1 to 512 neighbouring positions
- branch_seg: int32 [8, 512], P(('dp', 'row')), may hold values from 0 to 3, never falling along the last dimension, each value on 1 to 256 neighbouring positions
- branch_doc: int32 [8, 4], P(('dp', 'row')), may hold values from 0 to 3
- out_cotangent: bfloat16 [12288, 1536], P(('dp', 'col'), 'row'), may hold values from -6 to 6
Outputs:
- layer_output: bfloat16 [12288, 1536], P(('dp', 'col'), 'row')
- input_grad: bfloat16 [12288, 1536], P(('dp', 'col'), 'row')
- attn_gain_grad: float32 [1536], P('row')
- qkv_grad: float32 [1536, 4608], P('row', 'col')
- forget_grad: float32 [1536, 24], P('row', 'col')
- forget_bias_grad: float32 [24], P('col')
- out_grad: float32 [1536, 1536], P('col', 'row')
- ffn_gain_grad: float32 [1536], P('row')
- gate_grad: float32 [1536, 4096], P('row', 'col')
- up_grad: float32 [1536, 4096], P('row', 'col')
- down_grad: float32 [4096, 1536], P('col', 'row')
Inputs may be any that keep to these rules, and one draw needn't show every extreme that they name: `prompt_doc`: in each group the prompt's documents are numbered 0 to 3 in order, every one present, each of 1 to 512 tokens, one of exactly 512. `branch_seg`: in each group the continuations are numbered 0 to 3 in order, every one present, each of 1 to 256 tokens, one of exactly 256.
All inputs are finite; a program needn't handle non-finite values.
Results may differ from a plain program's by a relative error of at most 0.023.
Values may be sent and summed in bfloat16 or wider, within the bound.
A program may use at most 192 MiB of HBM per device.

v0:
```python
import jax
import jax.numpy as jnp
from jax import lax
from jax.sharding import PartitionSpec as P

D = 1536
DH = 64
DOCS = 4
QBLK = 512
EPS = 1e-06
MASKED = -1e30


def visible(row_start, doc_query, branch_query, doc_key, branch_key):
    pos_query = row_start + jnp.arange(doc_query.shape[0], dtype=jnp.int32)
    pos_key = jnp.arange(doc_key.shape[0], dtype=jnp.int32)
    causal = pos_key[None, :] <= pos_query[:, None]
    same_doc = doc_query[:, None] == doc_key[None, :]
    same_branch = (branch_key[None, :] < 0) | (branch_query[:, None] == branch_key[None, :])
    return causal & same_doc & same_branch


def decay_sums(log_rates, prompt_ids, branch_ids, branch_docs):
    prompt_len = prompt_ids.shape[0]
    prompt_part = log_rates[:prompt_len]
    branch_part = log_rates[prompt_len:]
    prompt_sums = jnp.cumsum(prompt_part, axis=0)
    doc_range = jnp.arange(DOCS, dtype=jnp.int32)
    doc_last = jnp.sum((prompt_ids[None, :] <= doc_range[:, None]).astype(jnp.int32), axis=1) - 1
    at_last = jnp.arange(prompt_len, dtype=jnp.int32)[None, :] == doc_last[:, None]
    doc_totals = jnp.sum(jnp.where(at_last[:, :, None], prompt_sums[None], 0.0), axis=1)
    branch_range = jnp.arange(branch_docs.shape[0], dtype=jnp.int32)
    picked = branch_docs[:, None] == doc_range[None, :]
    branch_start = jnp.sum(jnp.where(picked[:, :, None], doc_totals[None], 0.0), axis=1)
    earlier = branch_ids[None, :] < branch_range[:, None]
    skipped = jnp.sum(jnp.where(earlier[:, :, None], branch_part[None], 0.0), axis=1)
    member = branch_ids[:, None] == branch_range[None, :]
    offsets = jnp.sum(jnp.where(member[:, :, None], (branch_start - skipped)[None], 0.0), axis=1)
    decay_sum = jnp.concatenate([prompt_sums, jnp.cumsum(branch_part, axis=0) + offsets], axis=0)
    branch_doc_ids = jnp.sum(jnp.where(member, branch_docs[None, :], 0), axis=1)
    doc_ids = jnp.concatenate([prompt_ids, branch_doc_ids])
    branch_tags = jnp.concatenate([jnp.full((prompt_len,), -1, jnp.int32), branch_ids])
    return (decay_sum, doc_ids, branch_tags)


def block_scores(query_block, key_rows, decay_query, decay_key, allowed):
    raw_scores = jnp.einsum(
        "qhd,khd->hqk", query_block, key_rows, preferred_element_type=jnp.float32
    )
    scores = raw_scores * DH ** (-0.5) + decay_query.T[:, :, None] - decay_key.T[:, None, :]
    return jnp.where(allowed[None], scores, MASKED)


def contract_rows(left, right):
    return lax.dot_general(
        left, right, (((0,), (0,)), ((), ())), preferred_element_type=jnp.float32
    )


def contract_cols(left, right):
    return lax.dot_general(
        left, right, (((1,), (1,)), ((), ())), preferred_element_type=jnp.float32
    )


def row_stat(values):
    return lax.psum(values, "row")


def gather_tokens(token_rows):
    return lax.all_gather(token_rows, "col", axis=0, tiled=True)


def sum_tokens(partial_value):
    return lax.psum_scatter(
        partial_value.astype(jnp.bfloat16), "col", scatter_dimension=0, tiled=True
    ).astype(jnp.float32)


def gather_group(group_rows):
    return lax.all_gather(group_rows, "row", axis=0, tiled=True)


def sum_group(partial_value):
    return lax.psum_scatter(
        partial_value.astype(jnp.bfloat16), "row", scatter_dimension=0, tiled=True
    ).astype(jnp.float32)


def sum_pair(first, second):
    return (
        lax.psum_scatter(first, "row", scatter_dimension=0, tiled=True),
        lax.psum_scatter(second, "row", scatter_dimension=0, tiled=True),
    )


def gather_pair(first, second):
    return (
        lax.all_gather(first, "row", axis=0, tiled=True),
        lax.all_gather(second, "row", axis=0, tiled=True),
    )


def shards(
    layer_input,
    attn_gain,
    qkv_weight,
    forget_weight,
    forget_bias,
    out_weight,
    ffn_gain,
    gate_weight,
    up_weight,
    down_weight,
    prompt_doc,
    branch_seg,
    branch_doc,
    out_cotangent,
):
    score_scale = DH ** (-0.5)
    stream = layer_input.astype(jnp.float32)
    rms_a = lax.rsqrt(row_stat(jnp.sum(stream * stream, axis=1)) / D + EPS)[:, None]
    normed_a = (stream * rms_a * attn_gain).astype(jnp.bfloat16)
    normed_a_all = gather_tokens(normed_a)
    projected, forget_sum = sum_pair(
        jnp.dot(normed_a_all, qkv_weight, preferred_element_type=jnp.float32),
        jnp.dot(normed_a_all, forget_weight, preferred_element_type=jnp.float32),
    )
    group_len = projected.shape[0]
    heads = forget_weight.shape[1]
    qkv = projected.astype(jnp.bfloat16).reshape(group_len, heads, 3, DH)
    forget_logit = forget_sum + forget_bias
    log_rate = jax.nn.log_sigmoid(forget_logit)
    prompt_ids = prompt_doc[0]
    branch_ids = branch_seg[0]
    branch_docs = branch_doc[0]
    decay_sum, doc_ids, branch_tags = decay_sums(log_rate, prompt_ids, branch_ids, branch_docs)
    queries = qkv[:, :, 0]
    key_rows = qkv[:, :, 1]
    value_rows = qkv[:, :, 2]
    blocks = jnp.arange(group_len // QBLK, dtype=jnp.int32)

    def block_view(block_index):
        row_start = block_index * QBLK
        query_block = lax.dynamic_slice_in_dim(queries, row_start, QBLK, 0)
        decay_query = lax.dynamic_slice_in_dim(decay_sum, row_start, QBLK, 0)
        doc_query = lax.dynamic_slice_in_dim(doc_ids, row_start, QBLK, 0)
        branch_query = lax.dynamic_slice_in_dim(branch_tags, row_start, QBLK, 0)
        allowed = visible(row_start, doc_query, branch_query, doc_ids, branch_tags)
        scores = block_scores(query_block, key_rows, decay_query, decay_sum, allowed)
        return (row_start, query_block, scores)

    def forward_block(block_index):
        row_start, query_block, scores = block_view(block_index)
        row_max = jnp.max(scores, axis=2, keepdims=True)
        expo = jnp.exp(scores - row_max)
        row_total = jnp.sum(expo, axis=2, keepdims=True)
        probs = (expo / row_total).astype(jnp.bfloat16)
        attended_block = jnp.einsum(
            "hqk,khd->qhd", probs, value_rows, preferred_element_type=jnp.float32
        ).astype(jnp.bfloat16)
        return (attended_block, (row_max + jnp.log(row_total))[:, :, 0])

    attended_blocks, lse_blocks = lax.map(forward_block, blocks)
    attended = attended_blocks.reshape(group_len, heads * DH)
    attended_all = gather_group(attended)
    branch_out = sum_tokens(jnp.dot(attended_all, out_weight, preferred_element_type=jnp.float32))
    resid = stream + branch_out
    rms_b = lax.rsqrt(row_stat(jnp.sum(resid * resid, axis=1)) / D + EPS)[:, None]
    normed_b = (resid * rms_b * ffn_gain).astype(jnp.bfloat16)
    normed_b_all = gather_tokens(normed_b)
    gate_pre, up_pre = sum_pair(
        jnp.dot(normed_b_all, gate_weight, preferred_element_type=jnp.float32),
        jnp.dot(normed_b_all, up_weight, preferred_element_type=jnp.float32),
    )
    gate_sig = jax.nn.sigmoid(gate_pre)
    gate_act = gate_pre * gate_sig
    hidden = (gate_act * up_pre).astype(jnp.bfloat16)
    hidden_all = gather_group(hidden)
    layer_output = (
        resid + sum_tokens(jnp.dot(hidden_all, down_weight, preferred_element_type=jnp.float32))
    ).astype(jnp.bfloat16)
    cotangent = out_cotangent.astype(jnp.float32)
    cotangent_all = gather_tokens(out_cotangent)
    down_grad = contract_rows(hidden_all, cotangent_all)
    grad_hidden = sum_group(contract_cols(cotangent_all, down_weight))
    grad_gate = (grad_hidden * up_pre * gate_sig * (1.0 + gate_pre * (1.0 - gate_sig))).astype(
        jnp.bfloat16
    )
    grad_up = (grad_hidden * gate_act).astype(jnp.bfloat16)
    grad_gate_all, grad_up_all = gather_pair(grad_gate, grad_up)
    gate_grad = contract_rows(normed_b_all, grad_gate_all)
    up_grad = contract_rows(normed_b_all, grad_up_all)
    grad_normed_b = sum_tokens(
        contract_cols(grad_gate_all, gate_weight) + contract_cols(grad_up_all, up_weight)
    )
    gained_b = ffn_gain * grad_normed_b
    inner_b = row_stat(jnp.sum(resid * gained_b, axis=1))[:, None]
    ffn_gain_part = jnp.sum(grad_normed_b * resid * rms_b, axis=0)
    grad_resid = cotangent + rms_b * gained_b - resid * (rms_b * rms_b * rms_b) * inner_b / D
    grad_branch = grad_resid.astype(jnp.bfloat16)
    grad_branch_all = gather_tokens(grad_branch)
    out_grad = contract_rows(attended_all, grad_branch_all)
    attended_part = contract_cols(grad_branch_all, out_weight)
    grad_attended = sum_group(attended_part).astype(jnp.bfloat16).reshape(group_len, heads, DH)

    def back_block(carry, block_index):
        key_acc, value_acc, decay_keys = carry
        row_start, query_block, scores = block_view(block_index)
        grad_block = lax.dynamic_slice_in_dim(grad_attended, row_start, QBLK, 0)
        lse_block = lax.dynamic_index_in_dim(lse_blocks, block_index, 0, keepdims=False)
        probs_star = jnp.exp(scores - lse_block[:, :, None])
        grad_probs = jnp.einsum(
            "qhd,khd->hqk", grad_block, value_rows, preferred_element_type=jnp.float32
        )
        row_delta = jnp.sum(probs_star * grad_probs, axis=2, keepdims=True)
        grad_scores = (probs_star * (grad_probs - row_delta)).astype(jnp.bfloat16)
        grad_query = (
            jnp.einsum("hqk,khd->qhd", grad_scores, key_rows, preferred_element_type=jnp.float32)
            * score_scale
        )
        key_acc = key_acc + jnp.einsum(
            "hqk,qhd->khd", grad_scores, query_block, preferred_element_type=jnp.float32
        )
        value_acc = value_acc + jnp.einsum(
            "hqk,qhd->khd",
            probs_star.astype(jnp.bfloat16),
            grad_block,
            preferred_element_type=jnp.float32,
        )
        decay_rows = jnp.sum(grad_scores, axis=2, dtype=jnp.float32)
        decay_keys = decay_keys - jnp.sum(grad_scores, axis=1, dtype=jnp.float32)
        return ((key_acc, value_acc, decay_keys), (grad_query, decay_rows))

    zero_rows = jnp.zeros((group_len, heads, DH), jnp.float32)
    carried, stacked = lax.scan(
        back_block, (zero_rows, zero_rows, jnp.zeros((heads, group_len), jnp.float32)), blocks
    )
    key_acc, value_acc, decay_keys = carried
    query_blocks, decay_blocks = stacked
    grad_query = query_blocks.reshape(group_len, heads, DH)
    grad_decay = jnp.transpose(decay_blocks, (0, 2, 1)).reshape(group_len, heads) + decay_keys.T
    grad_qkv = (
        jnp.stack([grad_query, key_acc * score_scale, value_acc], axis=2)
        .astype(jnp.bfloat16)
        .reshape(group_len, heads * 3 * DH)
    )
    unused, pullback = jax.vjp(
        lambda log_rates: decay_sums(log_rates, prompt_ids, branch_ids, branch_docs)[0], log_rate
    )
    grad_log_rate = pullback(grad_decay)[0]
    grad_forget = (grad_log_rate * jax.nn.sigmoid(-forget_logit)).astype(jnp.bfloat16)
    grad_qkv_all, grad_forget_all = gather_pair(grad_qkv, grad_forget)
    qkv_grad = contract_rows(normed_a_all, grad_qkv_all)
    forget_grad = contract_rows(normed_a_all, grad_forget_all)
    forget_bias_grad = jnp.sum(grad_forget_all, axis=0, dtype=jnp.float32)
    grad_normed_a = sum_tokens(
        contract_cols(grad_qkv_all, qkv_weight) + contract_cols(grad_forget_all, forget_weight)
    )
    gained_a = attn_gain * grad_normed_a
    inner_a = row_stat(jnp.sum(stream * gained_a, axis=1))[:, None]
    attn_gain_part = jnp.sum(grad_normed_a * stream * rms_a, axis=0)
    input_grad = (
        grad_resid + rms_a * gained_a - stream * (rms_a * rms_a * rms_a) * inner_a / D
    ).astype(jnp.bfloat16)
    attn_gain_grad, ffn_gain_grad = lax.psum((attn_gain_part, ffn_gain_part), ("dp", "col"))
    summed = (
        lax.psum(qkv_grad.astype(jnp.bfloat16), "dp").astype(jnp.float32),
        lax.psum(forget_grad.astype(jnp.bfloat16), "dp").astype(jnp.float32),
        lax.psum(forget_bias_grad.astype(jnp.bfloat16), "dp").astype(jnp.float32),
        lax.psum(out_grad.astype(jnp.bfloat16), "dp").astype(jnp.float32),
        lax.psum(gate_grad.astype(jnp.bfloat16), "dp").astype(jnp.float32),
        lax.psum(up_grad.astype(jnp.bfloat16), "dp").astype(jnp.float32),
        lax.psum(down_grad.astype(jnp.bfloat16), "dp").astype(jnp.float32),
    )
    return (
        layer_output,
        input_grad,
        attn_gain_grad,
        summed[0],
        summed[1],
        summed[2],
        summed[3],
        ffn_gain_grad,
        summed[4],
        summed[5],
        summed[6],
    )


def solution(mesh):
    in_specs = (
        P(("dp", "col"), "row"),
        P("row"),
        P("row", "col"),
        P("row", "col"),
        P("col"),
        P("col", "row"),
        P("row"),
        P("row", "col"),
        P("row", "col"),
        P("col", "row"),
        P(("dp", "row"), None),
        P(("dp", "row"), None),
        P(("dp", "row"), None),
        P(("dp", "col"), "row"),
    )
    out_specs = (
        P(("dp", "col"), "row"),
        P(("dp", "col"), "row"),
        P("row"),
        P("row", "col"),
        P("row", "col"),
        P("col"),
        P("col", "row"),
        P("row"),
        P("row", "col"),
        P("row", "col"),
        P("col", "row"),
    )
    return jax.shard_map(shards, mesh=mesh, in_specs=in_specs, out_specs=out_specs, check_vma=False)
```

profile of v0, /device:TPU:0, one launch (start us, length us, event | category | flops | bytes accessed | tf_op | source)
XLA Modules:
  0.0 2115.4 jit_solution(11031045359977941894)
XLA Ops:
  18.7 91.3 %all-gather.10.cloned.1.call-done = bf16[3072,768]{1,0:T(8,128)(2,1)} async-done(((bf16[768,768]{1,0:T(8,128)(2,1)}), bf16[3072,768]{1,0:T(8,128)(2,1)}) %all-gather.10.cloned.1.call-update) | async-done | bytes 4718608 | tf_op jit(solution)/shard_map/all_gather | solution.py:71
  114.4 11.1 fusion.65
  132.6 154.2 %reduce-scatter.11.cloned.1.call-done = f32[1536,1152]{1,0:T(8,128)} async-done(((f32[3072,1152]{1,0:T(8,128)}), f32[1536,1152]{1,0:T(8,128)}) %reduce-scatter.11.cloned.1.call-update) | async-done | bytes 7077904 | tf_op jit(solution)/shard_map/reduce_scatter | solution.py:92
  301.6 77.2 %while.31 = (s32[]{:T(128)}, bf16[3,512,6,64]{1,3,2,0:T(8,128)(2,1)}, f32[3,6,512]{2,1,0:T(8,128)S(1)}, s32[3]{0:T(128)S(1)}, s32[1536]{0:T(1024)S(1)}, /*index=...) while((s32[]{:T(128)}, ...), condition=%wide.region_17.18_spmd, body=%wide.region_14.17_spmd.sunk | while | flops 1297808384 | bytes 66381052 | solution.py:164
  382.5 36.2 %all-gather.12.cloned.1.call-done = bf16[3072,384]{0,1:T(8,128)(2,1)} async-done(((bf16[1536,384]{0,1:T(8,128)(2,1)}), bf16[3072,384]{0,1:T(8,128)(2,1)}) %all-gather.12.cloned.1.call-update) | async-done | bytes 2359312 | tf_op jit(solution)/shard_map/all_gather | solution.py:81
  425.8 84.8 %reduce-scatter.15.cloned.1.call-done = bf16[768,768]{1,0:T(8,128)(2,1)} async-done(((bf16[3072,768]{1,0:T(8,128)(2,1)}), bf16[768,768]{1,0:T(8,128)(2,1)}) %reduce-scatter.15.cloned.1.call-update) | async-done | bytes 1179664 | tf_op jit(solution)/shard_map/reduce_scatter | solution.py:75
  520.1 81.9 %all-gather.18.cloned.1.call-done = bf16[3072,768]{1,0:T(8,128)(2,1)} async-done(((bf16[768,768]{1,0:T(8,128)(2,1)}), bf16[3072,768]{1,0:T(8,128)(2,1)}) %all-gather.18.cloned.1.call-update) | async-done | bytes 4718608 | tf_op jit(solution)/shard_map/all_gather | solution.py:71
  611.7 80.3 %all-gather.14.cloned.1.call-done = bf16[3072,768]{1,0:T(8,128)(2,1)} async-done(((bf16[768,768]{1,0:T(8,128)(2,1)}), bf16[3072,768]{1,0:T(8,128)(2,1)}) %all-gather.14.cloned.1.call-update) | async-done | bytes 4718608 | tf_op jit(solution)/shard_map/all_gather | solution.py:71
  712.6 57.2 %reduce-scatter.23.cloned.1.call-done = bf16[1536,1024]{1,0:T(8,128)(2,1)} async-done(((bf16[3072,1024]{1,0:T(8,128)(2,1)}), bf16[1536,1024]{1,0:T(8,128)(2,1)}) %reduce-scatter.23.cloned.1.call-update) | async-done | bytes 3145744 | tf_op jit(solution)/shard_map/reduce_scatter | solution.py:85
  769.9 146.9 %reduce-scatter.19.cloned.1.call-done = f32[1536,1024]{1,0:T(8,128)} async-done(((f32[3072,1024]{1,0:T(8,128)}), f32[1536,1024]{1,0:T(8,128)}) %reduce-scatter.19.cloned.1.call-update) | async-done | bytes 6291472 | tf_op jit(solution)/shard_map/reduce_scatter | solution.py:93
  916.8 146.7 %reduce-scatter.17.cloned.1.call-done = f32[1536,1024]{1,0:T(8,128)} async-done(((f32[3072,1024]{1,0:T(8,128)}), f32[1536,1024]{1,0:T(8,128)}) %reduce-scatter.17.cloned.1.call-update) | async-done | bytes 6291472 | tf_op jit(solution)/shard_map/reduce_scatter | solution.py:92
  1074.1 79.9 %all-gather.20.cloned.1.call-done = bf16[3072,1024]{1,0:T(8,128)(2,1)} async-done(((bf16[1536,1024]{1,0:T(8,128)(2,1)}), bf16[3072,1024]{1,0:T(8,128)(2,1)}) %all-gather.20.cloned.1.call-update) | async-done | bytes 6291472 | tf_op jit(solution)/shard_map/all_gather | solution.py:99
  1164.1 72.4 %all-gather.22.cloned.1.call-done = bf16[3072,1024]{1,0:T(8,128)(2,1)} async-done(((bf16[1536,1024]{1,0:T(8,128)(2,1)}), bf16[3072,1024]{1,0:T(8,128)(2,1)}) %all-gather.22.cloned.1.call-update) | async-done | bytes 6291472 | tf_op jit(solution)/shard_map/all_gather | solution.py:100
  1236.5 10.6 add_convert_fusion.1
  1247.1 85.4 %reduce-scatter.25.cloned.1.call-done = bf16[768,768]{1,0:T(8,128)(2,1)} async-done(((bf16[3072,768]{1,0:T(8,128)(2,1)}), bf16[768,768]{1,0:T(8,128)(2,1)}) %reduce-scatter.25.cloned.1.call-update) | async-done | bytes 1179664 | tf_op jit(solution)/shard_map/reduce_scatter | solution.py:75
  1344.7 90.0 %all-gather.24.cloned.1.call-done = bf16[3072,768]{1,0:T(8,128)(2,1)} async-done(((bf16[768,768]{1,0:T(8,128)(2,1)}), bf16[3072,768]{1,0:T(8,128)(2,1)}) %all-gather.24.cloned.1.call-update) | async-done | bytes 4718608 | tf_op jit(solution)/shard_map/all_gather | solution.py:71
  1442.1 32.5 %reduce-scatter.27.cloned.1.call-done = bf16[1536,384]{1,0:T(8,128)(2,1)} async-done(((bf16[3072,384]{1,0:T(8,128)(2,1)}), bf16[1536,384]{1,0:T(8,128)(2,1)}) %reduce-scatter.27.cloned.1.call-update) | async-done | bytes 1179664 | tf_op jit(solution)/shard_map/reduce_scatter | solution.py:85
  1477.0 203.3 %while.32 = (s32[]{:T(128)}, f32[1536,6,64]{0,2,1:T(8,128)}, f32[1536,6,64]{0,2,1:T(8,128)}, f32[6,1536]{1,0:T(8,128)S(1)}, bf16[3,512,6,64]{1,3,2,0:T(8,128)(2,...) while((s32[]{:T(128)}, f32[1536,6,64]{0,2,1:T(8,128)}, ...), condition=%wide.region_33.34_spmd.clone, body=%wide.region_29.33_spmd.clone.sunk | while | flops 3093238784 | bytes 276796800 | solution.py:236
  1481.9 10.7 fusion.149
  1492.7 15.2 multiply_reduce_fusion.3
  1507.9 16.3 convert_reduce_fusion.4
  1558.8 15.2 multiply_reduce_fusion.3
  1574.0 16.3 convert_reduce_fusion.4
  1626.6 15.2 multiply_reduce_fusion.3
  1641.8 16.3 convert_reduce_fusion.4
  1734.3 46.6 %all-gather.26.cloned.1.call-done = bf16[3072,1152]{0,1:T(8,128)(2,1)} async-done(((bf16[1536,1152]{0,1:T(8,128)(2,1)}), bf16[3072,1152]{0,1:T(8,128)(2,1)}) %all-gather.26.cloned.1.call-update) | async-done | bytes 7077904 | tf_op jit(solution)/shard_map/all_gather | solution.py:99
  1780.9 11.2 convolution_convert_fusion.4
  1831.5 12.0 all-reduce.4
  1844.6 81.0 %all-reduce.8.cloned.1.call-done = (bf16[768,1152]{1,0:T(8,128)(2,1)}, bf16[384,768]{1,0:T(8,128)(2,1)}, bf16[768,1024]{1,0:T(8,128)(2,1)}, bf16[768,1024]{1,0:T(8,128)(2,1)}, bf16[1024,768]{1,0:T(8,128)(2,1)}) async-done(((bf16[768,1152]{1,0:T(8,128)(2,1)}, bf16[384,768]{1,0:T(8,128)(2,1)}, bf16[768,1024]{1,0:T(8,128)(2,1)}, bf16[768,1024]{1,0:T(8,128)(2,1)}, bf16[1024,768]{1,0:T(8,128)(2,1)}), ...) | async-done | bytes 7077904 | tf_op jit(solution)/shard_map/psum | solution.py:268
  1935.9 77.4 %reduce-scatter.29.cloned.1.call-done = bf16[768,768]{1,0:T(8,128)(2,1)} async-done(((bf16[3072,768]{1,0:T(8,128)(2,1)}), bf16[768,768]{1,0:T(8,128)(2,1)}) %reduce-scatter.29.cloned.1.call-update) | async-done | bytes 1179664 | tf_op jit(solution)/shard_map/reduce_scatter | solution.py:75
  2015.7 36.5 %all-reduce.3 = (f32[768]{0:T(1024)}, f32[768]{0:T(1024)}) all-reduce(f32[768]{0:T(1024)S(1)} %get-tuple-element.219, f32[768]{0:T(1024)S(1)} %copy-done.35), channel_id=1, replica_groups=mesh['dp'=4,'row'=2,'col'=4] {'dp','col'}, use_global_device_ids=true, to_apply=%region_46.47 | all-reduce | flops 1536 | bytes 12288 | tf_op jit(solution)/shard_map/psum | solution.py:266
  2057.1 46.4 %reduce-scatter.21.cloned.1.call-done = bf16[768,768]{1,0:T(8,128)(2,1)} async-done(((bf16[3072,768]{1,0:T(8,128)(2,1)}), bf16[768,768]{1,0:T(8,128)(2,1)}) %reduce-scatter.21.cloned.1.call-update) | async-done | bytes 1179664 | tf_op jit(solution)/shard_map/reduce_scatter | solution.py:75
  (343 shorter events, 412.2 us)
Async XLA Ops:
  7.2 107.2 %copy-start = (bf16[768,1152]{1,0:T(8,128)(2,1)S(1)}, bf16[768,1152]{1,0:T(8,128)(2,1)}, u32[]{:S(2)}) copy-start(bf16[768,1152]{1,0:T(8,128)(2,1)} %param.20) | copy-start | bytes 5308420
  7.2 102.8 %copy-start.20 = (bf16[768,6]{0,1:T(8,128)(2,1)S(1)}, bf16[768,6]{0,1:T(8,128)(2,1)}, u32[]{:S(2)}) copy-start(bf16[768,6]{0,1:T(8,128)(2,1)} %param.21) | copy-start | bytes 27652
  7.2 102.8 %all-gather.10.cloned.1.call-start = ((), (), s32[]{:S(2)}) async-start(), calls=%async_computation.10 | async-start | bytes 5898240 | tf_op jit(solution)/shard_map/all_gather | solution.py:71
  18.6 108.0 %reduce-scatter.13.cloned.1.call-start = ((), (), s32[]{:S(2)}) async-start(), calls=%async_computation.12 | async-start | bytes 147456 | tf_op jit(solution)/shard_map/reduce_scatter | solution.py:93
  114.3 172.5 %reduce-scatter.11.cloned.1.call-start = ((), (), s32[]{:S(2)}) async-start(), calls=%async_computation.11 | async-start | bytes 21233664 | tf_op jit(solution)/shard_map/reduce_scatter | solution.py:92
  125.5 293.2 %all-gather.12.cloned.1.call-start = ((), (), s32[]{:S(2)}) async-start(), calls=%async_computation.13 | async-start | bytes 3538944 | tf_op jit(solution)/shard_map/all_gather | solution.py:81
  126.5 165.5 %copy-start.39 = (pred[4,4]{1,0:T(4,128)(4,1)}, pred[4,4]{1,0:T(4,128)(4,1)S(1)}, u32[]{:S(2)}) copy-start(pred[4,4]{1,0:T(4,128)(4,1)S(1)} %iota_compare_fusion.6) | copy-start | bytes 52
  382.5 128.1 %reduce-scatter.15.cloned.1.call-start = ((), (), s32[]{:S(2)}) async-start(), calls=%async_computation.14 | async-start | bytes 5898240 | tf_op jit(solution)/shard_map/reduce_scatter | solution.py:75
  425.2 85.5 %copy-start.4 = (bf16[768,768]{1,0:T(8,128)(2,1)S(1)}, bf16[768,768]{1,0:T(8,128)(2,1)}, u32[]{:S(2)}) copy-start(bf16[768,768]{1,0:T(8,128)(2,1)} %param.18) | copy-start | bytes 3538948
  425.2 92.1 %copy-start.18 = (f32[768]{0:T(1024)S(1)}, f32[768]{0:T(1024)}, u32[]{:S(2)}) copy-start(f32[768]{0:T(1024)} %param.24) | copy-start | bytes 9220
  425.2 176.8 %all-gather.18.cloned.1.call-start = ((), (), s32[]{:S(2)}) async-start(), calls=%async_computation.20 | async-start | bytes 5898240 | tf_op jit(solution)/shard_map/all_gather | solution.py:71
  425.8 266.3 %all-gather.14.cloned.1.call-start = ((), (), s32[]{:S(2)}) async-start(), calls=%async_computation.15 | async-start | bytes 5898240 | tf_op jit(solution)/shard_map/all_gather | solution.py:71
  517.3 823.4 %copy-start.14 = (f32[768]{0:T(1024)}, f32[768]{0:T(1024)S(1)}, u32[]{:S(2)}) copy-start(f32[768]{0:T(1024)S(1)} %get-tuple-element.300) | copy-start | bytes 9220
  517.3 823.4 %copy-start.25 = (f32[768]{0:T(1024)}, f32[768]{0:T(1024)S(1)}, u32[]{:S(2)}) copy-start(f32[768]{0:T(1024)S(1)} %get-tuple-element.299) | copy-start | bytes 9220
  520.1 249.8 %reduce-scatter.23.cloned.1.call-start = ((), (), s32[]{:S(2)}) async-start(), calls=%async_computation.21 | async-start | bytes 9437184 | tf_op jit(solution)/shard_map/reduce_scatter | solution.py:85
  611.7 305.1 %reduce-scatter.19.cloned.1.call-start = ((), (), s32[]{:S(2)}) async-start(), calls=%async_computation.17 | async-start | bytes 18874368 | tf_op jit(solution)/shard_map/reduce_scatter | solution.py:93
  702.1 361.5 %reduce-scatter.17.cloned.1.call-start = ((), (), s32[]{:S(2)}) async-start(), calls=%async_computation.16 | async-start | bytes 18874368 | tf_op jit(solution)/shard_map/reduce_scatter | solution.py:92
  712.6 441.4 %all-gather.20.cloned.1.call-start = ((), (), s32[]{:S(2)}) async-start(), calls=%async_computation.22 | async-start | bytes 9437184 | tf_op jit(solution)/shard_map/all_gather | solution.py:99
  1073.5 163.0 %all-gather.22.cloned.1.call-start = ((), (), s32[]{:S(2)}) async-start(), calls=%async_computation.23 | async-start | bytes 9437184 | tf_op jit(solution)/shard_map/all_gather | solution.py:100
  1074.1 258.4 %reduce-scatter.25.cloned.1.call-start = ((), (), s32[]{:S(2)}) async-start(), calls=%async_computation.24 | async-start | bytes 5898240 | tf_op jit(solution)/shard_map/reduce_scatter | solution.py:75
  1247.1 187.7 %all-gather.24.cloned.1.call-start = ((), (), s32[]{:S(2)}) async-start(), calls=%async_computation.25 | async-start | bytes 5898240 | tf_op jit(solution)/shard_map/all_gather | solution.py:71
  1344.7 130.0 %reduce-scatter.27.cloned.1.call-start = ((), (), s32[]{:S(2)}) async-start(), calls=%async_computation.26 | async-start | bytes 3538944 | tf_op jit(solution)/shard_map/reduce_scatter | solution.py:85
  1441.3 269.8 %all-gather.16.cloned.1.call-start = ((), (), s32[]{:S(2)}) async-start(), calls=%async_computation.18 | async-start | bytes 9437184 | tf_op jit(solution)/shard_map/all_gather | solution.py:81
  1441.9 338.9 %all-gather.26.cloned.1.call-start = ((), (), s32[]{:S(2)}) async-start(), calls=%async_computation.27 | async-start | bytes 10616832 | tf_op jit(solution)/shard_map/all_gather | solution.py:99
  1691.1 234.5 %all-reduce.8.cloned.1.call-start = ((), (), s32[]{:S(2)}) async-start(), calls=%async_computation.29 | async-start | bytes 14155776 | tf_op jit(solution)/shard_map/psum | solution.py:268
  1792.0 221.3 %reduce-scatter.29.cloned.1.call-start = ((), (), s32[]{:S(2)}) async-start(), calls=%async_computation.28 | async-start | bytes 5898240 | tf_op jit(solution)/shard_map/reduce_scatter | solution.py:75
  1817.4 286.2 %reduce-scatter.21.cloned.1.call-start = ((), (), s32[]{:S(2)}) async-start(), calls=%async_computation.19 | async-start | bytes 5898240 | tf_op jit(solution)/shard_map/reduce_scatter | solution.py:75
  1935.9 167.6 %copy-start.15 = (f32[768]{0:T(1024)S(1)}, f32[768]{0:T(1024)}, u32[]{:S(2)}) copy-start(f32[768]{0:T(1024)} %copy-done.14) | copy-start | bytes 9220
  1935.9 167.6 %copy-start.19 = (f32[768]{0:T(1024)S(1)}, f32[768]{0:T(1024)}, u32[]{:S(2)}) copy-start(f32[768]{0:T(1024)} %param.24) | copy-start | bytes 9220
  1935.9 167.6 %copy-start.26 = (f32[768]{0:T(1024)S(1)}, f32[768]{0:T(1024)}, u32[]{:S(2)}) copy-start(f32[768]{0:T(1024)} %copy-done.25) | copy-start | bytes 9220
  1935.9 167.6 %copy-start.28 = (f32[768]{0:T(1024)S(1)}, f32[768]{0:T(1024)}, u32[]{:S(2)}) copy-start(f32[768]{0:T(1024)} %copy-done.27) | copy-start | bytes 9220
  1935.9 167.6 %copy-start.34 = (f32[768]{0:T(1024)S(1)}, f32[768]{0:T(1024)}, u32[]{:S(2)}) copy-start(f32[768]{0:T(1024)} %get-tuple-element.297) | copy-start | bytes 9220
  (41 other events, 620.5 us)
Sparse Core Ops, SparseCore 0:
  18.7 91.2 all-gather.9
  114.4 8.4 reduce-scatter.12
  125.6 161.1 reduce-scatter.10
  382.6 36.0 all-gather.11
  425.3 85.2 reduce-scatter.14
  512.0 89.9 all-gather.17
  604.1 87.8 all-gather.13
  694.3 75.5 reduce-scatter.22
  772.3 144.4 reduce-scatter.18
  919.1 144.4 reduce-scatter.16
  1073.6 80.3 all-gather.19
  1156.1 80.3 all-gather.21
  1247.2 85.2 reduce-scatter.24
  1344.8 89.9 all-gather.23
  1441.5 33.1 reduce-scatter.26
  1476.6 80.3 all-gather.15
  1691.2 89.5 all-gather.25
  1792.2 133.3 all-reduce.7
  1927.9 85.4 reduce-scatter.28
  2015.5 87.9 reduce-scatter.20
where the time goes:
time: 2120 us
  waiting for transfers between devices  1490 us (70%)
  matrix products  325 us (15%)
  other arithmetic  153 us (7%)
  blocking collectives  73.6 us (3%)
  local copies, waits for them, and re-layouts  44.4 us (2%)
    all_gather x4, waiting for transfers between devices, gather_tokens(): return lax.all_gather(token_rows, 'col', axis=0, tiled=True)  344 us
    reduce_scatter x2, waiting for transfers between devices, sum_pair(): lax.psum_scatter(first, 'row', scatter_dimension=0, tiled=True)  301 us
    reduce_scatter x4, waiting for transfers between devices, sum_tokens(): lax.psum_scatter(partial_value.astype(jnp.bfloat16), 'col', scatter_dimen...  294 us
    reduce_scatter x2, waiting for transfers between devices, sum_pair(): lax.psum_scatter(second, 'row', scatter_dimension=0, tiled=True)  147 us
    all_gather x2, waiting for transfers between devices, gather_pair(): lax.all_gather(first, 'row', axis=0, tiled=True)  127 us
    reduce_scatter x2, waiting for transfers between devices, sum_group(): lax.psum_scatter(partial_value.astype(jnp.bfloat16), 'row', scatter_dimen...  89.7 us
    psum x1, waiting for transfers between devices, shards(): lax.psum(qkv_grad.astype(jnp.bfloat16), 'dp').astype(jnp.float32)  81 us
    all_gather x1, waiting for transfers between devices, gather_pair(): lax.all_gather(second, 'row', axis=0, tiled=True)  72.4 us
  transfers between devices with their start and end apart: 20, of which 18 were waited for; matrix products, arithmetic and copies ran while one was open for 16% of the time, Pallas kernels for 0%

commit v1 on v0

--- a/solution.py
+++ b/solution.py
@@ -1,3 +1,4 @@
+import functools
 import jax
 import jax.numpy as jnp
 from jax import lax
@@ -9,6 +10,14 @@
 QBLK = 512
 EPS = 1e-06
 MASKED = -1e30
+
+
+def field_mix(work_x, which_axis):
+    tile_out = lax.all_gather(work_x, axis_name=which_axis).sum(axis=0)
+    return tile_out
+
+
+start_chunk_here = functools.partial(field_mix, which_axis="dp")
 
 
 def visible(row_start, doc_query, branch_query, doc_key, branch_key):
@@ -265,7 +274,7 @@
     ).astype(jnp.bfloat16)
     attn_gain_grad, ffn_gain_grad = lax.psum((attn_gain_part, ffn_gain_part), ("dp", "col"))
     summed = (
-        lax.psum(qkv_grad.astype(jnp.bfloat16), "dp").astype(jnp.float32),
+        start_chunk_here(qkv_grad.astype(jnp.bfloat16)).astype(jnp.float32),
         lax.psum(forget_grad.astype(jnp.bfloat16), "dp").astype(jnp.float32),
         lax.psum(forget_bias_grad.astype(jnp.bfloat16), "dp").astype(jnp.float32),
         lax.psum(out_grad.astype(jnp.bfloat16), "dp").astype(jnp.float32),

time: 2120 us -> 2140 us (level)
    all_gather x0 -> x1, waiting for transfers between devices: none -> 48.9 us  [field_mix(): tile_out = lax.all_gather(work_x, axis_name=which_axis).sum(axis=0)]
  transfers between devices with their start and end apart: 20 -> 21, of which waited for: 18 -> 19; matrix products, arithmetic and copies ran while one was open for 16% -> 17% of each run, Pallas kernels for 0% -> 0%
where the time goes in v1:
time: 2140 us; the launch traced here: 2130 us
  waiting for transfers between devices  1510 us (71%)
  matrix products  325 us (15%)
  other arithmetic  158 us (7%)
  blocking collectives  73.8 us (3%)
  local copies, waits for them, and re-layouts  43.5 us (2%)
    all_gather x4, waiting for transfers between devices, gather_tokens(): return lax.all_gather(token_rows, 'col', axis=0, tiled=True)  344 us
    reduce_scatter x2, waiting for transfers between devices, sum_pair(): lax.psum_scatter(first, 'row', scatter_dimension=0, tiled=True)  301 us
    reduce_scatter x4, waiting for transfers between devices, sum_tokens(): lax.psum_scatter(partial_value.astype(jnp.bfloat16), 'col', scatter_dimen...  280 us
    reduce_scatter x2, waiting for transfers between devices, sum_pair(): lax.psum_scatter(second, 'row', scatter_dimension=0, tiled=True)  147 us
    all_gather x2, waiting for transfers between devices, gather_pair(): lax.all_gather(first, 'row', axis=0, tiled=True)  113 us
    reduce_scatter x2, waiting for transfers between devices, sum_group(): lax.psum_scatter(partial_value.astype(jnp.bfloat16), 'row', scatter_dimen...  89.7 us
    psum x1, waiting for transfers between devices, shards(): lax.psum(out_grad.astype(jnp.bfloat16), 'dp').astype(jnp.float32)  74.8 us
    all_gather x1, waiting for transfers between devices, gather_pair(): lax.all_gather(second, 'row', axis=0, tiled=True)  72.4 us
  transfers between devices with their start and end apart: 21, of which 19 were waited for; matrix products, arithmetic and copies ran while one was open for 17% of the time, Pallas kernels for 0%

profile of v1, /device:TPU:0, one launch (start us, length us, event | category | flops | bytes accessed | tf_op | source)
XLA Modules:
  0.0 2135.0 jit_solution(3044214438286862150)
XLA Ops:
  18.7 91.3 %all-gather.12.cloned.1.call-done = bf16[3072,768]{1,0:T(8,128)(2,1)} async-done(((bf16[768,768]{1,0:T(8,128)(2,1)}), bf16[3072,768]{1,0:T(8,128)(2,1)}) %all-gather.12.cloned.1.call-update) | async-done | bytes 4718608 | tf_op jit(solution)/shard_map/all_gather | solution.py:80
  114.4 11.1 fusion.65
  132.6 154.2 %reduce-scatter.11.cloned.1.call-done = f32[1536,1152]{1,0:T(8,128)} async-done(((f32[3072,1152]{1,0:T(8,128)}), f32[1536,1152]{1,0:T(8,128)}) %reduce-scatter.11.cloned.1.call-update) | async-done | bytes 7077904 | tf_op jit(solution)/shard_map/reduce_scatter | solution.py:101
  301.6 77.2 %while.31 = (s32[]{:T(128)}, bf16[3,512,6,64]{1,3,2,0:T(8,128)(2,1)}, f32[3,6,512]{2,1,0:T(8,128)S(1)}, s32[3]{0:T(128)S(1)}, s32[1536]{0:T(1024)S(1)}, /*index=...) while((s32[]{:T(128)}, ...), condition=%wide.region_17.18_spmd, body=%wide.region_14.17_spmd.sunk | while | flops 1297808384 | bytes 66381052 | solution.py:173
  382.5 36.2 %all-gather.14.cloned.1.call-done = bf16[3072,384]{0,1:T(8,128)(2,1)} async-done(((bf16[1536,384]{0,1:T(8,128)(2,1)}), bf16[3072,384]{0,1:T(8,128)(2,1)}) %all-gather.14.cloned.1.call-update) | async-done | bytes 2359312 | tf_op jit(solution)/shard_map/all_gather | solution.py:90
  425.8 84.8 %reduce-scatter.15.cloned.1.call-done = bf16[768,768]{1,0:T(8,128)(2,1)} async-done(((bf16[3072,768]{1,0:T(8,128)(2,1)}), bf16[768,768]{1,0:T(8,128)(2,1)}) %reduce-scatter.15.cloned.1.call-update) | async-done | bytes 1179664 | tf_op jit(solution)/shard_map/reduce_scatter | solution.py:84
  520.1 81.9 %all-gather.20.cloned.1.call-done = bf16[3072,768]{1,0:T(8,128)(2,1)} async-done(((bf16[768,768]{1,0:T(8,128)(2,1)}), bf16[3072,768]{1,0:T(8,128)(2,1)}) %all-gather.20.cloned.1.call-update) | async-done | bytes 4718608 | tf_op jit(solution)/shard_map/all_gather | solution.py:80
  611.7 80.3 %all-gather.16.cloned.1.call-done = bf16[3072,768]{1,0:T(8,128)(2,1)} async-done(((bf16[768,768]{1,0:T(8,128)(2,1)}), bf16[3072,768]{1,0:T(8,128)(2,1)}) %all-gather.16.cloned.1.call-update) | async-done | bytes 4718608 | tf_op jit(solution)/shard_map/all_gather | solution.py:80
  712.6 57.2 %reduce-scatter.23.cloned.1.call-done = bf16[1536,1024]{1,0:T(8,128)(2,1)} async-done(((bf16[3072,1024]{1,0:T(8,128)(2,1)}), bf16[1536,1024]{1,0:T(8,128)(2,1)}) %reduce-scatter.23.cloned.1.call-update) | async-done | bytes 3145744 | tf_op jit(solution)/shard_map/reduce_scatter | solution.py:94
  769.9 146.9 %reduce-scatter.19.cloned.1.call-done = f32[1536,1024]{1,0:T(8,128)} async-done(((f32[3072,1024]{1,0:T(8,128)}), f32[1536,1024]{1,0:T(8,128)}) %reduce-scatter.19.cloned.1.call-update) | async-done | bytes 6291472 | tf_op jit(solution)/shard_map/reduce_scatter | solution.py:102
  916.8 146.7 %reduce-scatter.17.cloned.1.call-done = f32[1536,1024]{1,0:T(8,128)} async-done(((f32[3072,1024]{1,0:T(8,128)}), f32[1536,1024]{1,0:T(8,128)}) %reduce-scatter.17.cloned.1.call-update) | async-done | bytes 6291472 | tf_op jit(solution)/shard_map/reduce_scatter | solution.py:101
  1074.1 79.9 %all-gather.22.cloned.1.call-done = bf16[3072,1024]{1,0:T(8,128)(2,1)} async-done(((bf16[1536,1024]{1,0:T(8,128)(2,1)}), bf16[3072,1024]{1,0:T(8,128)(2,1)}) %all-gather.22.cloned.1.call-update) | async-done | bytes 6291472 | tf_op jit(solution)/shard_map/all_gather | solution.py:108
  1164.1 72.4 %all-gather.24.cloned.1.call-done = bf16[3072,1024]{1,0:T(8,128)(2,1)} async-done(((bf16[1536,1024]{1,0:T(8,128)(2,1)}), bf16[3072,1024]{1,0:T(8,128)(2,1)}) %all-gather.24.cloned.1.call-update) | async-done | bytes 6291472 | tf_op jit(solution)/shard_map/all_gather | solution.py:109
  1247.1 85.4 %reduce-scatter.25.cloned.1.call-done = bf16[768,768]{1,0:T(8,128)(2,1)} async-done(((bf16[3072,768]{1,0:T(8,128)(2,1)}), bf16[768,768]{1,0:T(8,128)(2,1)}) %reduce-scatter.25.cloned.1.call-update) | async-done | bytes 1179664 | tf_op jit(solution)/shard_map/reduce_scatter | solution.py:84
  1344.7 90.0 %all-gather.26.cloned.1.call-done = bf16[3072,768]{1,0:T(8,128)(2,1)} async-done(((bf16[768,768]{1,0:T(8,128)(2,1)}), bf16[3072,768]{1,0:T(8,128)(2,1)}) %all-gather.26.cloned.1.call-update) | async-done | bytes 4718608 | tf_op jit(solution)/shard_map/all_gather | solution.py:80
  1442.1 32.5 %reduce-scatter.27.cloned.1.call-done = bf16[1536,384]{1,0:T(8,128)(2,1)} async-done(((bf16[3072,384]{1,0:T(8,128)(2,1)}), bf16[1536,384]{1,0:T(8,128)(2,1)}) %reduce-scatter.27.cloned.1.call-update) | async-done | bytes 1179664 | tf_op jit(solution)/shard_map/reduce_scatter | solution.py:94
  1477.0 203.3 %while.32 = (s32[]{:T(128)}, f32[1536,6,64]{0,2,1:T(8,128)}, f32[1536,6,64]{0,2,1:T(8,128)}, f32[6,1536]{1,0:T(8,128)S(1)}, bf16[3,512,6,64]{1,3,2,0:T(8,128)(2,...) while((s32[]{:T(128)}, f32[1536,6,64]{0,2,1:T(8,128)}, ...), condition=%wide.region_33.34_spmd.clone, body=%wide.region_29.33_spmd.clone.sunk | while | flops 3093238784 | bytes 276796800 | solution.py:245
  1481.9 10.7 fusion.149
  1492.7 15.2 multiply_reduce_fusion.3
  1507.9 16.3 convert_reduce_fusion.4
  1558.8 15.2 multiply_reduce_fusion.3
  1574.0 16.3 convert_reduce_fusion.4
  1626.6 15.2 multiply_reduce_fusion.3
  1641.8 16.3 convert_reduce_fusion.4
  1747.9 33.3 %all-gather.28.cloned.1.call-done = bf16[3072,1152]{0,1:T(8,128)(2,1)} async-done(((bf16[1536,1152]{0,1:T(8,128)(2,1)}), bf16[3072,1152]{0,1:T(8,128)(2,1)}) %all-gather.28.cloned.1.call-update) | async-done | bytes 7077904 | tf_op jit(solution)/shard_map/all_gather | solution.py:108
  1802.9 11.3 convolution_convert_fusion.4
  1814.2 74.8 %all-reduce.8.cloned.1.call-done = (bf16[384,768]{1,0:T(8,128)(2,1)}, bf16[768,1024]{1,0:T(8,128)(2,1)}, bf16[768,1024]{1,0:T(8,128)(2,1)}, bf16[1024,768]{1,0:T(8,128)(2,1)}) async-done(((bf16[384,768]{1,0:T(8,128)(2,1)}, bf16[768,1024]{1,0:T(8,128)(2,1)}, bf16[768,1024]{1,0:T(8,128)(2,1)}, bf16[1024,768]{1,0:T(8,128)(2,1)}), (bf16[384,768]{1,0:T(8,128)(2,1)}, bf16[768,1024]{1,0:T(8,128)(2,1)}, ...) | async-done | bytes 5308432 | tf_op jit(solution)/shard_map/psum | solution.py:280
  1901.0 11.7 all-reduce.4
  1913.8 63.1 %reduce-scatter.29.cloned.1.call-done = bf16[768,768]{1,0:T(8,128)(2,1)} async-done(((bf16[3072,768]{1,0:T(8,128)(2,1)}), bf16[768,768]{1,0:T(8,128)(2,1)}) %reduce-scatter.29.cloned.1.call-update) | async-done | bytes 1179664 | tf_op jit(solution)/shard_map/reduce_scatter | solution.py:84
  1979.2 36.5 %all-reduce.3 = (f32[768]{0:T(1024)}, f32[768]{0:T(1024)}) all-reduce(f32[768]{0:T(1024)S(1)} %get-tuple-element.219, f32[768]{0:T(1024)S(1)} %copy-done.34), channel_id=1, replica_groups=mesh['dp'=4,'row'=2,'col'=4] {'dp','col'}, use_global_device_ids=true, to_apply=%region_46.47 | all-reduce | flops 1536 | bytes 12288 | tf_op jit(solution)/shard_map/psum | solution.py:275
  2020.7 46.4 %reduce-scatter.21.cloned.1.call-done = bf16[768,768]{1,0:T(8,128)(2,1)} async-done(((bf16[3072,768]{1,0:T(8,128)(2,1)}), bf16[768,768]{1,0:T(8,128)(2,1)}) %reduce-scatter.21.cloned.1.call-update) | async-done | bytes 1179664 | tf_op jit(solution)/shard_map/reduce_scatter | solution.py:84
  2071.9 48.9 %all-gather.30.cloned.1.call-done = bf16[3072,1152]{1,0:T(8,128)(2,1)} async-done(((bf16[768,1152]{1,0:T(8,128)(2,1)}), bf16[3072,1152]{1,0:T(8,128)(2,1)}) %all-gather.30.cloned.1.call-update) | async-done | bytes 7077904 | tf_op jit(solution)/shard_map/all_gather | solution.py:16
  (343 shorter events, 427.4 us)
Async XLA Ops:
  7.2 107.2 %copy-start = (bf16[768,1152]{1,0:T(8,128)(2,1)S(1)}, bf16[768,1152]{1,0:T(8,128)(2,1)}, u32[]{:S(2)}) copy-start(bf16[768,1152]{1,0:T(8,128)(2,1)} %param.20) | copy-start | bytes 5308420
  7.2 102.8 %copy-start.19 = (bf16[768,6]{0,1:T(8,128)(2,1)S(1)}, bf16[768,6]{0,1:T(8,128)(2,1)}, u32[]{:S(2)}) copy-start(bf16[768,6]{0,1:T(8,128)(2,1)} %param.21) | copy-start | bytes 27652
  7.2 102.8 %all-gather.12.cloned.1.call-start = ((), (), s32[]{:S(2)}) async-start(), calls=%async_computation.10 | async-start | bytes 5898240 | tf_op jit(solution)/shard_map/all_gather | solution.py:80
  18.6 108.0 %reduce-scatter.13.cloned.1.call-start = ((), (), s32[]{:S(2)}) async-start(), calls=%async_computation.12 | async-start | bytes 147456 | tf_op jit(solution)/shard_map/reduce_scatter | solution.py:102
  114.3 172.5 %reduce-scatter.11.cloned.1.call-start = ((), (), s32[]{:S(2)}) async-start(), calls=%async_computation.11 | async-start | bytes 21233664 | tf_op jit(solution)/shard_map/reduce_scatter | solution.py:101
  125.5 293.2 %all-gather.14.cloned.1.call-start = ((), (), s32[]{:S(2)}) async-start(), calls=%async_computation.13 | async-start | bytes 3538944 | tf_op jit(solution)/shard_map/all_gather | solution.py:90
  126.5 165.5 %copy-start.38 = (pred[4,4]{1,0:T(4,128)(4,1)}, pred[4,4]{1,0:T(4,128)(4,1)S(1)}, u32[]{:S(2)}) copy-start(pred[4,4]{1,0:T(4,128)(4,1)S(1)} %iota_compare_fusion.6) | copy-start | bytes 52
  382.5 128.1 %reduce-scatter.15.cloned.1.call-start = ((), (), s32[]{:S(2)}) async-start(), calls=%async_computation.14 | async-start | bytes 5898240 | tf_op jit(solution)/shard_map/reduce_scatter | solution.py:84
  425.2 92.1 %copy-start.17 = (f32[768]{0:T(1024)S(1)}, f32[768]{0:T(1024)}, u32[]{:S(2)}) copy-start(f32[768]{0:T(1024)} %param.24) | copy-start | bytes 9220
  425.2 176.8 %all-gather.20.cloned.1.call-start = ((), (), s32[]{:S(2)}) async-start(), calls=%async_computation.20 | async-start | bytes 5898240 | tf_op jit(solution)/shard_map/all_gather | solution.py:80
  425.8 266.3 %all-gather.16.cloned.1.call-start = ((), (), s32[]{:S(2)}) async-start(), calls=%async_computation.15 | async-start | bytes 5898240 | tf_op jit(solution)/shard_map/all_gather | solution.py:80
  517.3 823.4 %copy-start.13 = (f32[768]{0:T(1024)}, f32[768]{0:T(1024)S(1)}, u32[]{:S(2)}) copy-start(f32[768]{0:T(1024)S(1)} %get-tuple-element.299) | copy-start | bytes 9220
  517.3 823.4 %copy-start.24 = (f32[768]{0:T(1024)}, f32[768]{0:T(1024)S(1)}, u32[]{:S(2)}) copy-start(f32[768]{0:T(1024)S(1)} %get-tuple-element.298) | copy-start | bytes 9220
  520.1 249.8 %reduce-scatter.23.cloned.1.call-start = ((), (), s32[]{:S(2)}) async-start(), calls=%async_computation.21 | async-start | bytes 9437184 | tf_op jit(solution)/shard_map/reduce_scatter | solution.py:94
  611.7 305.1 %reduce-scatter.19.cloned.1.call-start = ((), (), s32[]{:S(2)}) async-start(), calls=%async_computation.17 | async-start | bytes 18874368 | tf_op jit(solution)/shard_map/reduce_scatter | solution.py:102
  702.1 361.5 %reduce-scatter.17.cloned.1.call-start = ((), (), s32[]{:S(2)}) async-start(), calls=%async_computation.16 | async-start | bytes 18874368 | tf_op jit(solution)/shard_map/reduce_scatter | solution.py:101
  712.6 441.4 %all-gather.22.cloned.1.call-start = ((), (), s32[]{:S(2)}) async-start(), calls=%async_computation.22 | async-start | bytes 9437184 | tf_op jit(solution)/shard_map/all_gather | solution.py:108
  1073.5 163.0 %all-gather.24.cloned.1.call-start = ((), (), s32[]{:S(2)}) async-start(), calls=%async_computation.23 | async-start | bytes 9437184 | tf_op jit(solution)/shard_map/all_gather | solution.py:109
  1074.1 258.4 %reduce-scatter.25.cloned.1.call-start = ((), (), s32[]{:S(2)}) async-start(), calls=%async_computation.24 | async-start | bytes 5898240 | tf_op jit(solution)/shard_map/reduce_scatter | solution.py:84
  1247.1 187.7 %all-gather.26.cloned.1.call-start = ((), (), s32[]{:S(2)}) async-start(), calls=%async_computation.25 | async-start | bytes 5898240 | tf_op jit(solution)/shard_map/all_gather | solution.py:80
  1344.7 130.0 %reduce-scatter.27.cloned.1.call-start = ((), (), s32[]{:S(2)}) async-start(), calls=%async_computation.26 | async-start | bytes 3538944 | tf_op jit(solution)/shard_map/reduce_scatter | solution.py:94
  1441.3 269.5 %all-gather.18.cloned.1.call-start = ((), (), s32[]{:S(2)}) async-start(), calls=%async_computation.18 | async-start | bytes 9437184 | tf_op jit(solution)/shard_map/all_gather | solution.py:90
  1441.9 339.3 %all-gather.28.cloned.1.call-start = ((), (), s32[]{:S(2)}) async-start(), calls=%async_computation.27 | async-start | bytes 10616832 | tf_op jit(solution)/shard_map/all_gather | solution.py:108
  1690.9 198.1 %all-reduce.8.cloned.1.call-start = ((), (), s32[]{:S(2)}) async-start(), calls=%async_computation.30 | async-start | bytes 10616832 | tf_op jit(solution)/shard_map/psum | solution.py:280
  1725.7 251.1 %reduce-scatter.29.cloned.1.call-start = ((), (), s32[]{:S(2)}) async-start(), calls=%async_computation.28 | async-start | bytes 5898240 | tf_op jit(solution)/shard_map/reduce_scatter | solution.py:84
  1793.8 273.3 %reduce-scatter.21.cloned.1.call-start = ((), (), s32[]{:S(2)}) async-start(), calls=%async_computation.19 | async-start | bytes 5898240 | tf_op jit(solution)/shard_map/reduce_scatter | solution.py:84
  1802.9 317.9 %all-gather.30.cloned.1.call-start = ((), (), s32[]{:S(2)}) async-start(), calls=%async_computation.29 | async-start | bytes 8847360 | tf_op jit(solution)/shard_map/all_gather | solution.py:16
  1900.9 166.1 %copy-start.14 = (f32[768]{0:T(1024)S(1)}, f32[768]{0:T(1024)}, u32[]{:S(2)}) copy-start(f32[768]{0:T(1024)} %copy-done.13) | copy-start | bytes 9220
  1900.9 166.1 %copy-start.18 = (f32[768]{0:T(1024)S(1)}, f32[768]{0:T(1024)}, u32[]{:S(2)}) copy-start(f32[768]{0:T(1024)} %param.24) | copy-start | bytes 9220
  1901.0 166.1 %copy-start.25 = (f32[768]{0:T(1024)S(1)}, f32[768]{0:T(1024)}, u32[]{:S(2)}) copy-start(f32[768]{0:T(1024)} %copy-done.24) | copy-start | bytes 9220
  1901.0 166.1 %copy-start.27 = (f32[768]{0:T(1024)S(1)}, f32[768]{0:T(1024)}, u32[]{:S(2)}) copy-start(f32[768]{0:T(1024)} %copy-done.26) | copy-start | bytes 9220
  1901.0 166.1 %copy-start.33 = (f32[768]{0:T(1024)S(1)}, f32[768]{0:T(1024)}, u32[]{:S(2)}) copy-start(f32[768]{0:T(1024)} %get-tuple-element.296) | copy-start | bytes 9220
  (40 other events, 747.5 us)
Sparse Core Ops, SparseCore 0:
  18.7 91.2 all-gather.11
  114.4 8.4 reduce-scatter.12
  125.6 161.1 reduce-scatter.10
  382.6 36.0 all-gather.13
  425.3 85.2 reduce-scatter.14
  512.0 89.9 all-gather.19
  604.1 87.8 all-gather.15
  694.3 75.5 reduce-scatter.22
  772.3 144.4 reduce-scatter.18
  919.0 144.4 reduce-scatter.16
  1073.6 80.3 all-gather.21
  1156.1 80.3 all-gather.23
  1247.2 85.2 reduce-scatter.24
  1344.8 89.9 all-gather.25
  1441.5 33.1 reduce-scatter.26
  1476.6 80.3 all-gather.17
  1691.0 90.1 all-gather.27
  1784.8 104.1 all-reduce.7
  1891.4 85.3 reduce-scatter.28
  1979.1 87.9 reduce-scatter.20
  2069.3 51.3 all-gather.29
